TPU v7x, 32 devices: a whole 2x2x4 slice. The times are simulated.
32 devices in a mesh: dp: 8 (over z, y), expert: 4 (over x, core).
Axes of the slice: x: 2, y: 2, z: 4, core: 2. Of those that a mesh axis runs over, the one named last changes fastest.
Arguments:
- tokens: bfloat16 [4096, 1024], P(('dp', 'expert')), may hold values from -6 to 6
- cotangent: bfloat16 [4096, 1024], P(('dp', 'expert')), may hold values from -6 to 6
- expert_ids: int32 [4096, 2], P(('dp', 'expert')), may hold values from 0 to 3, all different within a row; in each aligned block of 128 rows (0 to 127, 128 to 255, ...) at most 128 rows name the same one
- gate_weights: float32 [4096, 2], P(('dp', 'expert')), may hold values from 0.05 to 1
- w_gate: bfloat16 [4, 384, 1024], P('expert'), may hold values from -0.1875 to 0.1875
- w_up: bfloat16 [4, 384, 1024], P('expert'), may hold values from -0.1875 to 0.1875
- w_down: bfloat16 [4, 384, 1024], P('expert'), may hold values from -0.3125 to 0.3125
Outputs:
- layer_out: bfloat16 [4096, 1024], P(('dp', 'expert'))
- grad_tokens: bfloat16 [4096, 1024], P(('dp', 'expert'))
- grad_up: float32 [4, 384, 1024], P('expert', 'dp')
- grad_down: float32 [4, 384, 1024], P('expert', 'dp')
Inputs may be any that keep to these rules, and one draw needn't show every extreme that they name: `expert_ids`: each row names 2 different experts. Among the 128 rows of one device no expert is named more than 128 times, and in every draw some expert is named exactly 128 times by the rows of some device.
All inputs are finite; a program needn't handle non-finite values.
Results may differ from a plain program's by a relative error of at most 0.0065.
Values may be sent and summed in bfloat16 or wider, within the bound.
A program may use at most 64 MiB of HBM per device.

v0:
```python
import jax
import jax.numpy as jnp
from jax import lax
from jax.sharding import PartitionSpec as P


def batched(left_op, right_op, left_dim, right_dim):
    return lax.dot_general(
        left_op,
        right_op,
        (((left_dim,), (right_dim,)), ((0,), (0,))),
        preferred_element_type=jnp.float32,
    )


def forward(received, w_gate, w_up, w_down):
    gate_pre = batched(received, w_gate, 2, 2)
    up_pre = batched(received, w_up, 2, 2)
    gate_sig = jax.nn.sigmoid(gate_pre)
    hidden = (gate_pre * gate_sig * up_pre).astype(jnp.bfloat16)
    expert_out = batched(hidden, w_down, 2, 1).astype(jnp.bfloat16)
    return ((gate_pre, up_pre, gate_sig, hidden), expert_out)


def backward(received, grad_out, saved_acts, w_gate, w_up, w_down):
    gate_pre, up_pre, gate_sig, hidden = saved_acts
    grad_lower = lax.psum_scatter(
        batched(hidden, grad_out, 1, 1), "dp", scatter_dimension=1, tiled=True
    )
    grad_hidden = batched(grad_out, w_down, 2, 2)
    grad_up_pre = (grad_hidden * gate_pre * gate_sig).astype(jnp.bfloat16)
    grad_gate_pre = (grad_hidden * up_pre * gate_sig * (1.0 + gate_pre * (1.0 - gate_sig))).astype(
        jnp.bfloat16
    )
    grad_input = (batched(grad_gate_pre, w_gate, 2, 1) + batched(grad_up_pre, w_up, 2, 1)).astype(
        jnp.bfloat16
    )
    grad_upper = batched(grad_up_pre, received, 1, 1)
    grad_upper = lax.psum_scatter(grad_upper, "dp", scatter_dimension=1, tiled=True)
    return (grad_input, (grad_upper, grad_lower))


def shards(tokens, cotangent, expert_ids, gate_weights, w_gate, w_up, w_down):
    tok_rows, model_width = tokens.shape
    top_count = expert_ids.shape[1]
    local_experts = w_gate.shape[0]
    groups = lax.axis_size("expert")
    experts = local_experts * groups
    capacity = 2 * tok_rows * top_count // experts
    pair_count = tok_rows * top_count
    slot_count = experts * capacity
    flat_ids = expert_ids.reshape(-1)
    flat_gates = gate_weights.reshape(-1)
    onehot = (flat_ids[:, None] == jnp.arange(experts, dtype=jnp.int32)[None, :]).astype(jnp.int32)
    before = jnp.cumsum(onehot, axis=0) - onehot
    slot_rank = jnp.sum(before * onehot, axis=1)
    position = flat_ids * capacity + slot_rank
    matches = position[None, :] == jnp.arange(slot_count, dtype=jnp.int32)[:, None]
    source = (
        jnp.sum(jnp.where(matches, jnp.arange(pair_count, dtype=jnp.int32)[None, :] + 1, 0), axis=1)
        - 1
    )
    filled = source >= 0
    clipped = jnp.maximum(source, 0)
    token_rows = clipped // top_count
    slot_gates = jnp.where(filled, flat_gates[clipped], 0.0)
    sent_tokens = jnp.where(filled[:, None], tokens[token_rows], jnp.zeros((), jnp.bfloat16))
    sent_tokens = sent_tokens.reshape(experts, capacity, model_width)
    sent_grads = (slot_gates[:, None] * cotangent[token_rows].astype(jnp.float32)).astype(
        jnp.bfloat16
    )
    sent_grads = sent_grads.reshape(experts, capacity, model_width)
    received = lax.all_to_all(sent_tokens, "expert", split_axis=0, concat_axis=1, tiled=True)
    saved_acts, expert_out = forward(received, w_gate, w_up, w_down)
    back_out = lax.all_to_all(expert_out, "expert", split_axis=1, concat_axis=0, tiled=True)
    grad_out = lax.all_to_all(sent_grads, "expert", split_axis=0, concat_axis=1, tiled=True)
    grad_input, grads = backward(received, grad_out, saved_acts, w_gate, w_up, w_down)
    back_grad = lax.all_to_all(grad_input, "expert", split_axis=1, concat_axis=0, tiled=True)
    out_rows = (
        back_out.reshape(slot_count, model_width)[position].astype(jnp.float32)
        * flat_gates[:, None]
    )
    layer_out = jnp.sum(out_rows.reshape(tok_rows, top_count, model_width), axis=1).astype(
        jnp.bfloat16
    )
    grad_rows = back_grad.reshape(slot_count, model_width)[position].astype(jnp.float32)
    grad_tokens = jnp.sum(grad_rows.reshape(tok_rows, top_count, model_width), axis=1).astype(
        jnp.bfloat16
    )
    grad_scale = (tok_rows * lax.axis_size("dp") * groups * top_count / experts) ** (-0.5)
    return (layer_out, grad_tokens, grads[0] * grad_scale, grads[1] * grad_scale)


def solution(mesh):
    in_specs = (
        P(("dp", "expert"), None),
        P(("dp", "expert"), None),
        P(("dp", "expert"), None),
        P(("dp", "expert"), None),
        P("expert", None, None),
        P("expert", None, None),
        P("expert", None, None),
    )
    out_specs = (
        P(("dp", "expert"), None),
        P(("dp", "expert"), None),
        P("expert", "dp", None),
        P("expert", "dp", None),
    )
    return jax.shard_map(shards, mesh=mesh, in_specs=in_specs, out_specs=out_specs, check_vma=False)
```

profile of v0, /device:TPU:0, one launch (start us, length us, event | category | flops | bytes accessed | tf_op | source)
XLA Modules:
  0.0 203.4 jit_solution(15513453985991420824)
XLA Ops:
  11.1 3.5 %gather_fusion.2 = f32[512]{0:T(512)S(1)} fusion(f32[256]{0:T(256)S(1)} %reshape.257, s32[1024]{0:T(1024)S(1)} %pad_clamp_fusion), kind=kCustom, calls=%fused_computation.2 | custom fusion | bytes 6144 | tf_op jit(solution)/shard_map/gather | solution.py:66
  14.7 2.1 %gather_fusion = bf16[512,1024]{1,0:T(8,128)(2,1)S(1)} fusion(bf16[128,1024]{1,0:T(8,128)(2,1)S(1)} %copy-done.1, s32[1024]{0:T(1024)S(1)} %pad_clamp_fusion.2), kind=kCustom, calls=%fused_computation | custom fusion | bytes 2099200 | tf_op jit(solution)/shard_map/gather | solution.py:67
  18.0 4.2 %all-to-all-start = ((bf16[4,128,1024]{2,1,0:T(8,128)(2,1)}), bf16[4,128,1024]{2,1,0:T(8,128)(2,1)S(1)}, u32[]{:S(2)}, u32[]{:S(2)}) async-start(bf16[4,128,1024]{2,1,0:T(8,128)(2,1)} %broadcast_select_fusion), calls=%async_computation | async-start | bytes 2097152 | tf_op jit(solution)/shard_map/all_to_all | solution.py:73
  22.2 2.0 %gather_fusion.3 = bf16[512,1024]{1,0:T(8,128)(2,1)S(1)} fusion(bf16[128,1024]{1,0:T(8,128)(2,1)S(1)} %copy-done.2, s32[1024]{0:T(1024)S(1)} %pad_clamp_fusion.2), kind=kCustom, calls=%fused_computation.3 | custom fusion | bytes 2099200 | tf_op jit(solution)/shard_map/gather | solution.py:69
  25.5 11.1 %all-to-all-done = bf16[4,128,1024]{2,1,0:T(8,128)(2,1)S(1)} async-done(((bf16[4,128,1024]{2,1,0:T(8,128)(2,1)}), bf16[4,128,1024]{2,1,0:T(8,128)(2,1)S(1)}, u32[]{:S(2)}, u32[]{:S(2)}) %all-to-all-start) | async-done | bytes 1048608 | tf_op jit(solution)/shard_map/all_to_all | solution.py:73
  36.6 3.5 %all-to-all-start.2 = ((bf16[4,128,1024]{2,1,0:T(8,128)(2,1)}), bf16[4,128,1024]{2,1,0:T(8,128)(2,1)S(1)}, u32[]{:S(2)}, u32[]{:S(2)}) async-start(bf16[4,128,1024]{2,1,0:T(8,128)(2,1)} %fusion), calls=%async_computation.2 | async-start | bytes 2097152 | tf_op jit(solution)/shard_map/all_to_all | solution.py:76
  40.2 2.9 %fusion.11 = f32[512,384]{1,0:T(8,128)} fusion(bf16[512,1024]{1,0:T(8,128)(2,1)S(1)} %bitcast.83, bf16[1,384,1024]{2,1,0:T(8,128)(2,1)} %param.11), kind=kOutput, calls=%fused_computation.25 | convolution fusion | flops 402653184 | bytes 2621440 | tf_op jit(solution)/shard_map/dot_general | solution.py:8
  44.7 9.8 %all-to-all-done.2 = bf16[4,128,1024]{2,1,0:T(8,128)(2,1)S(1)} async-done(((bf16[4,128,1024]{2,1,0:T(8,128)(2,1)}), bf16[4,128,1024]{2,1,0:T(8,128)(2,1)S(1)}, u32[]{:S(2)}, u32[]{:S(2)}) %all-to-all-start.2) | async-done | bytes 1048608 | tf_op jit(solution)/shard_map/all_to_all | solution.py:76
  54.5 3.0 %multiply_convert_fusion = (bf16[512,384]{1,0:T(8,128)(2,1)S(1)}, bf16[512,384]{1,0:T(8,128)(2,1)S(1)}, f32[512,384]{1,0:T(8,128)}) fusion(f32[512,384]{1,0:T(8,128)} %fusion.11, f32[512,384]{1,0:T(8,128)} %fusion.7, bf16[512,1024]{1,0:T(8,128)(2,1)S(1)} %bitcast.92, bf16[1,384,1024]{2,1,0:T(8,128)(2,1)S(1)} %copy-done), kind=kOutput, calls=%fused_computation.27 | convolution fusion | flops 404422656 | bytes 4980736 | tf_op jit(solution)/shard_map/dot_general | solution.py:8
  62.1 2.6 %fusion.9 = f32[512,1024]{1,0:T(8,128)S(1)} fusion(bf16[1,384,1024]{2,1,0:T(8,128)(2,1)S(1)} %copy-done.7, f32[512,384]{1,0:T(8,128)} %fusion.11, f32[512,384]{1,0:T(8,128)} %get-tuple-element.10, f32[512,384]{1,0:T(8,128)} %fusion.7), kind=kOutput, calls=%fused_computation.23 | convolution fusion | flops 404619264 | bytes 5242880 | tf_op jit(solution)/shard_map/dot_general | solution.py:8
  67.6 7.8 %reduce.2 = bf16[512,1024]{1,0:T(8,128)(2,1)} reduce(bf16[512,1,1024]{2,1,0:T(2,128)(2,1)S(1)} %bitcast.88, bf16[]{:T(256)} %broadcast.255), dimensions={1}, to_apply=%bitcast.79.reduce_sub_computation | reduce | bytes 2097154
  75.4 3.8 %reshape.318 = bf16[4,2,65536]{2,1,0:T(2,128)(2,1)} reshape(bf16[512,1024]{1,0:T(8,128)(2,1)} %reduce.2) | data formatting | bytes 2097152
  79.2 4.5 %all-to-all-start.3 = ((bf16[4,2,65536]{2,1,0:T(2,128)(2,1)}), bf16[4,2,65536]{2,1,0:T(2,128)(2,1)}, u32[]{:S(2)}, u32[]{:S(2)}) async-start(bf16[4,2,65536]{2,1,0:T(2,128)(2,1)} %reshape.318), calls=%async_computation.3 | async-start | bytes 2097152 | tf_op jit(solution)/shard_map/all_to_all | solution.py:78
  86.0 7.8 %reduce.1 = bf16[512,1024]{1,0:T(8,128)(2,1)} reduce(bf16[512,1,1024]{2,1,0:T(2,128)(2,1)S(1)} %bitcast.89, bf16[]{:T(256)} %broadcast.255), dimensions={1}, to_apply=%bitcast.80.reduce_sub_computation | reduce | bytes 2097154
  93.8 3.7 %reshape.316 = bf16[4,2,65536]{2,1,0:T(2,128)(2,1)} reshape(bf16[512,1024]{1,0:T(8,128)(2,1)} %reduce.1) | data formatting | bytes 2097152
  97.9 3.8 %all-to-all-start.1 = ((bf16[4,2,65536]{2,1,0:T(2,128)(2,1)}), bf16[4,2,65536]{2,1,0:T(2,128)(2,1)S(1)}, u32[]{:S(2)}, u32[]{:S(2)}) async-start(bf16[4,2,65536]{2,1,0:T(2,128)(2,1)} %reshape.316), calls=%async_computation.1 | async-start | bytes 2097152 | tf_op jit(solution)/shard_map/all_to_all | solution.py:75
  102.0 4.0 %reshape.319 = bf16[512,1,1024]{2,1,0:T(2,128)(2,1)} reshape(bf16[4,2,65536]{2,1,0:T(2,128)(2,1)} %all-to-all-done.3) | data formatting | bytes 2097152
  106.0 2.0 copy.56
  109.4 6.5 %all-to-all-done.1 = bf16[4,2,65536]{2,1,0:T(2,128)(2,1)S(1)} async-done(((bf16[4,2,65536]{2,1,0:T(2,128)(2,1)}), bf16[4,2,65536]{2,1,0:T(2,128)(2,1)S(1)}, u32[]{:S(2)}, u32[]{:S(2)}) %all-to-all-start.1) | async-done | bytes 1048608 | tf_op jit(solution)/shard_map/all_to_all | solution.py:75
  115.9 2.3 %reshape.317 = bf16[512,1,1024]{2,1,0:T(2,128)(2,1)} reshape(bf16[4,2,65536]{2,1,0:T(2,128)(2,1)S(1)} %all-to-all-done.1) | data formatting | bytes 2097152
  118.2 2.0 copy.57
  122.0 2.1 %reduce_sum.45 = bf16[128,1024]{1,0:T(8,128)(2,1)} reduce(bf16[128,2,1024]{2,1,0:T(2,128)(2,1)S(1)} %gather.28, bf16[]{:T(256)} %constant.37.clone.1), dimensions={1}, to_apply=%region_5.6 | reduce | flops 131072 | bytes 786434 | tf_op jit(solution)/shard_map/reduce_sum | solution.py:87
  124.1 2.1 %multiply_reduce_fusion = bf16[128,1024]{1,0:T(8,128)(2,1)} fusion(f32[128,2,1024]{2,1,0:T(2,128)S(1)} %reshape.260, f32[128,2]{1,0:T(8,128)S(1)} %copy.45), kind=kLoop, calls=%fused_computation.15 | loop fusion | flops 393216 | bytes 1311744 | tf_op jit(solution)/shard_map/reduce_sum | solution.py:83
  128.7 66.2 %reduce-scatter.3.cloned.1.call-done = f32[1,48,1024]{2,1,0:T(8,128)} async-done(((f32[1,384,1024]{2,1,0:T(8,128)}), f32[1,48,1024]{2,1,0:T(8,128)}) %reduce-scatter.3.cloned.1.call-update) | async-done | bytes 196624 | tf_op jit(solution)/shard_map/reduce_scatter | solution.py:39
  (67 shorter events, 25.8 us)
Async XLA Ops:
  7.2 47.4 %copy-start = (bf16[1,384,1024]{2,1,0:T(8,128)(2,1)S(1)}, bf16[1,384,1024]{2,1,0:T(8,128)(2,1)}, u32[]{:S(2)}) copy-start(bf16[1,384,1024]{2,1,0:T(8,128)(2,1)} %param.13) | copy-start | bytes 2359300
  7.2 7.5 %copy-start.1 = (bf16[128,1024]{1,0:T(8,128)(2,1)S(1)}, bf16[128,1024]{1,0:T(8,128)(2,1)}, u32[]{:S(2)}) copy-start(bf16[128,1024]{1,0:T(8,128)(2,1)} %param.7) | copy-start | bytes 786436
  16.8 5.4 %copy-start.2 = (bf16[128,1024]{1,0:T(8,128)(2,1)S(1)}, bf16[128,1024]{1,0:T(8,128)(2,1)}, u32[]{:S(2)}) copy-start(bf16[128,1024]{1,0:T(8,128)(2,1)} %param.8) | copy-start | bytes 786436
  18.0 18.7 %all-to-all-start = ((bf16[4,128,1024]{2,1,0:T(8,128)(2,1)}), bf16[4,128,1024]{2,1,0:T(8,128)(2,1)S(1)}, u32[]{:S(2)}, u32[]{:S(2)}) async-start(bf16[4,128,1024]{2,1,0:T(8,128)(2,1)} %broadcast_select_fusion), calls=%async_computation | async-start | bytes 2097152 | tf_op jit(solution)/shard_map/all_to_all | solution.py:73
  36.6 17.9 %all-to-all-start.2 = ((bf16[4,128,1024]{2,1,0:T(8,128)(2,1)}), bf16[4,128,1024]{2,1,0:T(8,128)(2,1)S(1)}, u32[]{:S(2)}, u32[]{:S(2)}) async-start(bf16[4,128,1024]{2,1,0:T(8,128)(2,1)} %fusion), calls=%async_computation.2 | async-start | bytes 2097152 | tf_op jit(solution)/shard_map/all_to_all | solution.py:76
  40.1 86.9 %reduce-scatter.5.cloned.1.call-start = ((), (), s32[]{:S(2)}) async-start(), calls=%async_computation.7 | async-start | bytes 1769472 | tf_op jit(solution)/shard_map/reduce_scatter | solution.py:27
  40.2 2.9 %copy-start.3 = (bf16[1,384,1024]{2,1,0:T(8,128)(2,1)S(1)}, bf16[1,384,1024]{2,1,0:T(8,128)(2,1)}, u32[]{:S(2)}) copy-start(bf16[1,384,1024]{2,1,0:T(8,128)(2,1)} %param.12) | copy-start | bytes 2359300
  57.5 0.8 copy-start.5
  60.1 134.8 %reduce-scatter.3.cloned.1.call-start = ((), (), s32[]{:S(2)}) async-start(), calls=%async_computation.6 | async-start | bytes 1769472 | tf_op jit(solution)/shard_map/reduce_scatter | solution.py:39
  60.3 1.8 copy-start.7
  62.1 2.6 %copy-start.4 = (bf16[1,384,1024]{2,1,0:T(8,128)(2,1)S(1)}, bf16[1,384,1024]{2,1,0:T(8,128)(2,1)}, u32[]{:S(2)}) copy-start(bf16[1,384,1024]{2,1,0:T(8,128)(2,1)} %param.12) | copy-start | bytes 2359300
  75.4 8.3 %copy-start.6 = (bf16[512,384]{1,0:T(8,128)(2,1)S(1)}, bf16[512,384]{1,0:T(8,128)(2,1)}, u32[]{:S(2)}) copy-start(bf16[512,384]{1,0:T(8,128)(2,1)} %copy-done.5) | copy-start | bytes 1179652
  79.2 18.8 %all-to-all-start.3 = ((bf16[4,2,65536]{2,1,0:T(2,128)(2,1)}), bf16[4,2,65536]{2,1,0:T(2,128)(2,1)}, u32[]{:S(2)}, u32[]{:S(2)}) async-start(bf16[4,2,65536]{2,1,0:T(2,128)(2,1)} %reshape.318), calls=%async_computation.3 | async-start | bytes 2097152 | tf_op jit(solution)/shard_map/all_to_all | solution.py:78
  93.8 7.9 %copy-start.8 = (s32[128,2]{0,1:T(2,128)S(1)}, s32[128,2]{0,1:T(2,128)}, u32[]{:S(2)}) copy-start(s32[128,2]{0,1:T(2,128)} %param.9) | copy-start | bytes 3076
  97.9 17.9 %all-to-all-start.1 = ((bf16[4,2,65536]{2,1,0:T(2,128)(2,1)}), bf16[4,2,65536]{2,1,0:T(2,128)(2,1)S(1)}, u32[]{:S(2)}, u32[]{:S(2)}) async-start(bf16[4,2,65536]{2,1,0:T(2,128)(2,1)} %reshape.316), calls=%async_computation.1 | async-start | bytes 2097152 | tf_op jit(solution)/shard_map/all_to_all | solution.py:75
Sparse Core Ops, SparseCore 0:
  60.2 66.8 reduce-scatter.4
  130.5 64.3 reduce-scatter.2
where the time goes:
time: 204 us; the launch traced here: 203 us
  waiting for transfers between devices  95 us (47%)
  local copies, waits for them, and re-layouts  35.7 us (18%)
  other arithmetic  27 us (13%)
  starting transfers between devices  16.3 us (8%)
  matrix products  15 us (7%)
  between operations  14.3 us (7%)
    reduce_scatter x1, waiting for transfers between devices, backward(): lax.psum_scatter(grad_upper, 'dp', scatter_dimension=1, tiled=True)  66.2 us
    unnamed x27, local copies, waits for them, and re-layouts  20.8 us
    unnamed x3, other arithmetic  15.7 us
    dot_general x8, matrix products, batched(): lax.dot_general(left_op, right_op, (((left_dim,), (right_dim,)), ((0,), (...  15 us
    all_to_all x1, waiting for transfers between devices, shards(): lax.all_to_all(sent_tokens, 'expert', split_axis=0, concat_axis=1, tiled=...  11.1 us
    all_to_all x1, waiting for transfers between devices, shards(): lax.all_to_all(sent_grads, 'expert', split_axis=0, concat_axis=1, tiled=T...  9.83 us
    all_to_all x1, waiting for transfers between devices, shards(): lax.all_to_all(expert_out, 'expert', split_axis=1, concat_axis=0, tiled=T...  6.51 us
    all_to_all x1, starting transfers between devices, shards(): lax.all_to_all(grad_input, 'expert', split_axis=1, concat_axis=0, tiled=T...  4.48 us
  transfers between devices with their start and end apart: 6, of which 6 were waited for; matrix products, arithmetic and copies ran while one was open for 29% of the time, Pallas kernels for 0%

commit v1 on v0

--- a/solution.py
+++ b/solution.py
@@ -70,7 +70,18 @@
         jnp.bfloat16
     )
     sent_grads = sent_grads.reshape(experts, capacity, model_width)
-    received = lax.all_to_all(sent_tokens, "expert", split_axis=0, concat_axis=1, tiled=True)
+    ways, here = (lax.axis_size("expert"), lax.axis_index("expert"))
+    width = sent_tokens.shape[0] // ways
+    shape = list(sent_tokens.shape)
+    shape[0] = width
+    height = shape[1]
+    shape[1] = height * ways
+    received = jnp.zeros(shape, sent_tokens.dtype)
+    for mask in range(ways):
+        part = lax.dynamic_slice_in_dim(sent_tokens, (here ^ mask) * width, width, axis=0)
+        if mask:
+            part = lax.ppermute(part, "expert", [(d, d ^ mask) for d in range(ways)])
+        received = lax.dynamic_update_slice_in_dim(received, part, (here ^ mask) * height, axis=1)
     saved_acts, expert_out = forward(received, w_gate, w_up, w_down)
     back_out = lax.all_to_all(expert_out, "expert", split_axis=1, concat_axis=0, tiled=True)
     grad_out = lax.all_to_all(sent_grads, "expert", split_axis=0, concat_axis=1, tiled=True)

time: 204 us -> 194 us (0.951)
  waiting for transfers between devices: 95 us -> 81.6 us
  local copies, waits for them, and re-layouts: 35.7 us -> 40 us
    reduce_scatter x1, waiting for transfers between devices: 0.94 us -> 66.2 us  [backward(): lax.psum_scatter(batched(hidden, grad_out, 1, 1), 'dp', scatter_dimension...]
    reduce_scatter x1, waiting for transfers between devices: 66.2 us -> 2.13 us  [backward(): lax.psum_scatter(grad_upper, 'dp', scatter_dimension=1, tiled=True)]
    all_to_all x1 -> x0, waiting for transfers between devices: 11.1 us -> none  [shards(): lax.all_to_all(sent_tokens, 'expert', split_axis=0, concat_axis=1, tiled=...]
    all_to_all x1 -> x0, starting transfers between devices: 4.24 us -> none  [shards(): lax.all_to_all(sent_tokens, 'expert', split_axis=0, concat_axis=1, tiled=...]
    dynamic_update_slice x0 -> x4, local copies, waits for them, and re-layouts: none -> 3.96 us  [shards(): lax.dynamic_update_slice_in_dim(received, part, (here ^ mask) * height, a...]
    all_to_all x1, waiting for transfers between devices: 9.83 us -> 5.91 us  [shards(): lax.all_to_all(sent_grads, 'expert', split_axis=0, concat_axis=1, tiled=T...]
    ppermute x0 -> x3, starting transfers between devices: none -> 3.08 us  [shards(): part = lax.ppermute(part, 'expert', [(d, d ^ mask) for d in range(ways)])]
    ppermute x0 -> x3, waiting for transfers between devices: none -> 2.55 us  [shards(): part = lax.ppermute(part, 'expert', [(d, d ^ mask) for d in range(ways)])]
  transfers between devices with their start and end apart: 6 -> 8, of which waited for: 6 -> 6; matrix products, arithmetic and copies ran while one was open for 29% -> 34% of each run, Pallas kernels for 0% -> 0%
where the time goes in v1:
time: 194 us; the launch traced here: 193 us
  waiting for transfers between devices  81.6 us (42%)
  local copies, waits for them, and re-layouts  40 us (21%)
  other arithmetic  26 us (13%)
  matrix products  16.1 us (8%)
  starting transfers between devices  15.1 us (8%)
  between operations  14.4 us (7%)
    reduce_scatter x1, waiting for transfers between devices, backward(): lax.psum_scatter(batched(hidden, grad_out, 1, 1), 'dp', scatter_dimension...  66.2 us
    unnamed x27, local copies, waits for them, and re-layouts  20 us
    dot_general x8, matrix products, batched(): lax.dot_general(left_op, right_op, (((left_dim,), (right_dim,)), ((0,), (...  16.1 us
    unnamed x3, other arithmetic  15.7 us
    all_to_all x1, waiting for transfers between devices, shards(): lax.all_to_all(sent_grads, 'expert', split_axis=0, concat_axis=1, tiled=T...  5.91 us
    all_to_all x1, starting transfers between devices, shards(): lax.all_to_all(grad_input, 'expert', split_axis=1, concat_axis=0, tiled=T...  4.48 us
    all_to_all x1, waiting for transfers between devices, shards(): lax.all_to_all(expert_out, 'expert', split_axis=1, concat_axis=0, tiled=T...  4.42 us
    dynamic_update_slice x4, local copies, waits for them, and re-layouts, shards(): lax.dynamic_update_slice_in_dim(received, part, (here ^ mask) * height, a...  3.96 us
  transfers between devices with their start and end apart: 8, of which 6 were waited for; matrix products, arithmetic and copies ran while one was open for 34% of the time, Pallas kernels for 0%

profile of v1, /device:TPU:0, one launch (start us, length us, event | category | flops | bytes accessed | tf_op | source)
XLA Modules:
  0.0 193.3 jit_solution(18035983641127385782)
XLA Ops:
  11.1 3.5 %gather_fusion.2 = f32[512]{0:T(512)S(1)} fusion(f32[256]{0:T(256)S(1)} %reshape.268, s32[1024]{0:T(1024)S(1)} %pad_clamp_fusion), kind=kCustom, calls=%fused_computation.2 | custom fusion | bytes 6144 | tf_op jit(solution)/shard_map/gather | solution.py:66
  14.7 2.1 %gather_fusion = bf16[512,1024]{1,0:T(8,128)(2,1)S(1)} fusion(bf16[128,1024]{1,0:T(8,128)(2,1)S(1)} %copy-done.1, s32[1024]{0:T(1024)S(1)} %pad_clamp_fusion.2), kind=kCustom, calls=%fused_computation | custom fusion | bytes 2099200 | tf_op jit(solution)/shard_map/gather | solution.py:67
  18.4 2.5 %collective-permute-start.1 = (bf16[1,128,1024]{2,1,0:T(8,128)(2,1)}, bf16[1,128,1024]{2,1,0:T(8,128)(2,1)}, u32[]{:S(2)}, u32[]{:S(2)}) collective-permute-start(bf16[1,128,1024]{2,1,0:T(8,128)(2,1)} %get-tuple-element.7), channel_id=1, source_target_pairs={{0,2},{1,3},{2,0},{3,1},{4,6},{5,7},{6,4},{7,5},{8,10},{9,11},{10,... | collective-permute-start | bytes 786440 | tf_op jit(solution)/shard_map/ppermute | solution.py:83
  21.0 2.0 %gather_fusion.3 = bf16[512,1024]{1,0:T(8,128)(2,1)S(1)} fusion(bf16[128,1024]{1,0:T(8,128)(2,1)S(1)} %copy-done.2, s32[1024]{0:T(1024)S(1)} %pad_clamp_fusion.2), kind=kCustom, calls=%fused_computation.3 | custom fusion | bytes 2099200 | tf_op jit(solution)/shard_map/gather | solution.py:69
  24.3 3.5 %all-to-all-start.1 = ((bf16[4,128,1024]{2,1,0:T(8,128)(2,1)}), bf16[4,128,1024]{2,1,0:T(8,128)(2,1)S(1)}, u32[]{:S(2)}, u32[]{:S(2)}) async-start(bf16[4,128,1024]{2,1,0:T(8,128)(2,1)} %fusion), calls=%async_computation.1 | async-start | bytes 2097152 | tf_op jit(solution)/shard_map/all_to_all | solution.py:87
  31.1 2.5 %collective-permute-done.2 = bf16[1,128,1024]{2,1,0:T(8,128)(2,1)} collective-permute-done((bf16[1,128,1024]{2,1,0:T(8,128)(2,1)S(1)}, bf16[1,128,1024]{2,1,0:T(8,128)(2,1)}, u32[]{:S(2)}, u32[]{:S(2)}) %collective-permute-start.2) | collective-permute-done | bytes 262176 | tf_op jit(solution)/shard_map/ppermute | solution.py:83
  34.6 2.8 %fusion.11 = f32[512,384]{1,0:T(8,128)} fusion(bf16[512,1024]{1,0:T(8,128)(2,1)S(1)} %bitcast_dynamic-update-slice_fusion, bf16[1,384,1024]{2,1,0:T(8,128)(2,1)} %param.11), kind=kOutput, calls=%fused_computation.25 | convolution fusion | flops 402653184 | bytes 2621440 | tf_op jit(solution)/shard_map/dot_general | solution.py:8
  39.0 5.9 %all-to-all-done.1 = bf16[4,128,1024]{2,1,0:T(8,128)(2,1)S(1)} async-done(((bf16[4,128,1024]{2,1,0:T(8,128)(2,1)}), bf16[4,128,1024]{2,1,0:T(8,128)(2,1)S(1)}, u32[]{:S(2)}, u32[]{:S(2)}) %all-to-all-start.1) | async-done | bytes 1048608 | tf_op jit(solution)/shard_map/all_to_all | solution.py:87
  45.0 3.1 %multiply_convert_fusion = (bf16[512,384]{1,0:T(8,128)(2,1)S(1)}, bf16[512,384]{1,0:T(8,128)(2,1)}, f32[512,384]{1,0:T(8,128)}) fusion(f32[512,384]{1,0:T(8,128)} %fusion.11, f32[512,384]{1,0:T(8,128)} %fusion.7, bf16[512,1024]{1,0:T(8,128)(2,1)S(1)} %bitcast.96, bf16[1,384,1024]{2,1,0:T(8,128)(2,1)S(1)} %copy-done), kind=kOutput, calls=%fused_computation.27 | convolution fusion | flops 404422656 | bytes 4980736 | tf_op jit(solution)/shard_map/dot_general | solution.py:8
  50.1 2.8 %convolution_bitcast_fusion = f32[1,384,1024]{2,1,0:T(8,128)} fusion(bf16[512,384]{1,0:T(8,128)(2,1)} %get-tuple-element.10, bf16[512,1024]{1,0:T(8,128)(2,1)S(1)} %bitcast.97), kind=kOutput, calls=%fused_computation.8 | convolution fusion | flops 402653184 | bytes 3014656 | tf_op jit(solution)/shard_map/dot_general | solution.py:8
  53.0 2.6 %fusion.9 = f32[512,1024]{1,0:T(8,128)S(1)} fusion(bf16[1,384,1024]{2,1,0:T(8,128)(2,1)S(1)} %copy-done.7, f32[512,384]{1,0:T(8,128)} %fusion.11, f32[512,384]{1,0:T(8,128)} %get-tuple-element.13, f32[512,384]{1,0:T(8,128)} %fusion.7), kind=kOutput, calls=%fused_computation.23 | convolution fusion | flops 404619264 | bytes 5242880 | tf_op jit(solution)/shard_map/dot_general | solution.py:8
  58.4 7.8 %reduce.2 = bf16[512,1024]{1,0:T(8,128)(2,1)} reduce(bf16[512,1,1024]{2,1,0:T(2,128)(2,1)S(1)} %bitcast.92, bf16[]{:T(256)} %broadcast.260), dimensions={1}, to_apply=%bitcast.86.reduce_sub_computation | reduce | bytes 2097154
  66.2 3.8 %reshape.329 = bf16[4,2,65536]{2,1,0:T(2,128)(2,1)} reshape(bf16[512,1024]{1,0:T(8,128)(2,1)} %reduce.2) | data formatting | bytes 2097152
  70.0 4.5 %all-to-all-start.2 = ((bf16[4,2,65536]{2,1,0:T(2,128)(2,1)}), bf16[4,2,65536]{2,1,0:T(2,128)(2,1)}, u32[]{:S(2)}, u32[]{:S(2)}) async-start(bf16[4,2,65536]{2,1,0:T(2,128)(2,1)} %reshape.329), calls=%async_computation.2 | async-start | bytes 2097152 | tf_op jit(solution)/shard_map/all_to_all | solution.py:89
  76.8 7.8 %reduce.1 = bf16[512,1024]{1,0:T(8,128)(2,1)} reduce(bf16[512,1,1024]{2,1,0:T(2,128)(2,1)S(1)} %bitcast.93, bf16[]{:T(256)} %broadcast.260), dimensions={1}, to_apply=%bitcast.87.reduce_sub_computation | reduce | bytes 2097154
  84.7 3.7 %reshape.327 = bf16[4,2,65536]{2,1,0:T(2,128)(2,1)} reshape(bf16[512,1024]{1,0:T(8,128)(2,1)} %reduce.1) | data formatting | bytes 2097152
  88.8 3.8 %all-to-all-start = ((bf16[4,2,65536]{2,1,0:T(2,128)(2,1)}), bf16[4,2,65536]{2,1,0:T(2,128)(2,1)S(1)}, u32[]{:S(2)}, u32[]{:S(2)}) async-start(bf16[4,2,65536]{2,1,0:T(2,128)(2,1)} %reshape.327), calls=%async_computation | async-start | bytes 2097152 | tf_op jit(solution)/shard_map/all_to_all | solution.py:86
  92.9 4.0 %reshape.330 = bf16[512,1,1024]{2,1,0:T(2,128)(2,1)} reshape(bf16[4,2,65536]{2,1,0:T(2,128)(2,1)} %all-to-all-done.2) | data formatting | bytes 2097152
  100.2 2.1 %reduce_sum.45 = bf16[128,1024]{1,0:T(8,128)(2,1)} reduce(bf16[128,2,1024]{2,1,0:T(2,128)(2,1)S(1)} %gather.28, bf16[]{:T(256)} %constant.21.clone.1), dimensions={1}, to_apply=%region_5.6 | reduce | flops 131072 | bytes 786434 | tf_op jit(solution)/shard_map/reduce_sum | solution.py:98
  102.3 4.4 %all-to-all-done = bf16[4,2,65536]{2,1,0:T(2,128)(2,1)S(1)} async-done(((bf16[4,2,65536]{2,1,0:T(2,128)(2,1)}), bf16[4,2,65536]{2,1,0:T(2,128)(2,1)S(1)}, u32[]{:S(2)}, u32[]{:S(2)}) %all-to-all-start) | async-done | bytes 1048608 | tf_op jit(solution)/shard_map/all_to_all | solution.py:86
  106.7 2.3 %reshape.328 = bf16[512,1,1024]{2,1,0:T(2,128)(2,1)} reshape(bf16[4,2,65536]{2,1,0:T(2,128)(2,1)S(1)} %all-to-all-done) | data formatting | bytes 2097152
  112.8 2.1 %multiply_reduce_fusion = bf16[128,1024]{1,0:T(8,128)(2,1)} fusion(f32[128,2,1024]{2,1,0:T(2,128)S(1)} %reshape.271, f32[128,2]{1,0:T(8,128)S(1)} %copy.45), kind=kLoop, calls=%fused_computation.15 | loop fusion | flops 393216 | bytes 1311744 | tf_op jit(solution)/shard_map/reduce_sum | solution.py:94
  114.9 2.1 %reduce-scatter.3.cloned.1.call-done = f32[1,48,1024]{2,1,0:T(8,128)} async-done(((f32[1,384,1024]{2,1,0:T(8,128)}), f32[1,48,1024]{2,1,0:T(8,128)}) %reduce-scatter.3.cloned.1.call-update) | async-done | bytes 196624 | tf_op jit(solution)/shard_map/reduce_scatter | solution.py:39
  118.6 66.2 %reduce-scatter.5.cloned.1.call-done = f32[1,48,1024]{2,1,0:T(8,128)} async-done(((f32[1,384,1024]{2,1,0:T(8,128)}), f32[1,48,1024]{2,1,0:T(8,128)}) %reduce-scatter.5.cloned.1.call-update) | async-done | bytes 196624 | tf_op jit(solution)/shard_map/reduce_scatter | solution.py:27
  (77 shorter events, 30.9 us)
Async XLA Ops:
  7.2 37.8 %copy-start = (bf16[1,384,1024]{2,1,0:T(8,128)(2,1)S(1)}, bf16[1,384,1024]{2,1,0:T(8,128)(2,1)}, u32[]{:S(2)}) copy-start(bf16[1,384,1024]{2,1,0:T(8,128)(2,1)} %param.13) | copy-start | bytes 2359300
  7.2 7.5 %copy-start.1 = (bf16[128,1024]{1,0:T(8,128)(2,1)S(1)}, bf16[128,1024]{1,0:T(8,128)(2,1)}, u32[]{:S(2)}) copy-start(bf16[128,1024]{1,0:T(8,128)(2,1)} %param.7) | copy-start | bytes 786436
  16.8 4.3 %copy-start.2 = (bf16[128,1024]{1,0:T(8,128)(2,1)S(1)}, bf16[128,1024]{1,0:T(8,128)(2,1)}, u32[]{:S(2)}) copy-start(bf16[128,1024]{1,0:T(8,128)(2,1)} %param.8) | copy-start | bytes 786436
  16.9 6.2 %copy-start.3 = (bf16[4,128,1024]{2,1,0:T(8,128)(2,1)}, bf16[4,128,1024]{2,1,0:T(8,128)(2,1)S(1)}, u32[]{:S(2)}) copy-start(bf16[4,128,1024]{2,1,0:T(8,128)(2,1)S(1)} %broadcast_select_fusion) | copy-start | bytes 3145732
  17.9 11.1 %collective-permute-start = (bf16[1,128,1024]{2,1,0:T(8,128)(2,1)}, bf16[1,128,1024]{2,1,0:T(8,128)(2,1)}, u32[]{:S(2)}, u32[]{:S(2)}) collective-permute-start(bf16[1,128,1024]{2,1,0:T(8,128)(2,1)} %get-tuple-element.8), channel_id=1, source_target_pairs={{0,1},{1,0},{2,3},{3,2},{4,5},{5,4},{6,7},{7,6},{8,9},{9,8},{10,11... | collective-permute-start | bytes 786440 | tf_op jit(solution)/shard_map/ppermute | solution.py:83
  18.4 11.7 %collective-permute-start.1 = (bf16[1,128,1024]{2,1,0:T(8,128)(2,1)}, bf16[1,128,1024]{2,1,0:T(8,128)(2,1)}, u32[]{:S(2)}, u32[]{:S(2)}) collective-permute-start(bf16[1,128,1024]{2,1,0:T(8,128)(2,1)} %get-tuple-element.7), channel_id=1, source_target_pairs={{0,2},{1,3},{2,0},{3,1},{4,6},{5,7},{6,4},{7,5},{8,10},{9,11},{10,... | collective-permute-start | bytes 786440 | tf_op jit(solution)/shard_map/ppermute | solution.py:83
  20.9 12.7 %collective-permute-start.2 = (bf16[1,128,1024]{2,1,0:T(8,128)(2,1)S(1)}, bf16[1,128,1024]{2,1,0:T(8,128)(2,1)}, u32[]{:S(2)}, u32[]{:S(2)}) collective-permute-start(bf16[1,128,1024]{2,1,0:T(8,128)(2,1)S(1)} %get-tuple-element.6), channel_id=1, source_target_pairs={{0,3},{1,2},{2,1},{3,0},{4,7},{5,6},{6,5},{7,4},{8,11},{9,10},{10,... | collective-permute-start | bytes 786440 | tf_op jit(solution)/shard_map/ppermute | solution.py:83
  24.3 20.6 %all-to-all-start.1 = ((bf16[4,128,1024]{2,1,0:T(8,128)(2,1)}), bf16[4,128,1024]{2,1,0:T(8,128)(2,1)S(1)}, u32[]{:S(2)}, u32[]{:S(2)}) async-start(bf16[4,128,1024]{2,1,0:T(8,128)(2,1)} %fusion), calls=%async_computation.1 | async-start | bytes 2097152 | tf_op jit(solution)/shard_map/all_to_all | solution.py:87
  27.9 89.2 %reduce-scatter.3.cloned.1.call-start = ((), (), s32[]{:S(2)}) async-start(), calls=%async_computation.5 | async-start | bytes 1769472 | tf_op jit(solution)/shard_map/reduce_scatter | solution.py:39
  29.0 8.4 %copy-start.4 = (bf16[1,384,1024]{2,1,0:T(8,128)(2,1)S(1)}, bf16[1,384,1024]{2,1,0:T(8,128)(2,1)}, u32[]{:S(2)}) copy-start(bf16[1,384,1024]{2,1,0:T(8,128)(2,1)} %param.12) | copy-start | bytes 2359300
  49.9 134.9 %reduce-scatter.5.cloned.1.call-start = ((), (), s32[]{:S(2)}) async-start(), calls=%async_computation.6 | async-start | bytes 1769472 | tf_op jit(solution)/shard_map/reduce_scatter | solution.py:27
  50.1 2.9 %copy-start.7 = (bf16[1,384,1024]{2,1,0:T(8,128)(2,1)S(1)}, bf16[1,384,1024]{2,1,0:T(8,128)(2,1)}, u32[]{:S(2)}) copy-start(bf16[1,384,1024]{2,1,0:T(8,128)(2,1)} %param.11) | copy-start | bytes 2359300
  53.0 2.6 %copy-start.5 = (bf16[1,384,1024]{2,1,0:T(8,128)(2,1)S(1)}, bf16[1,384,1024]{2,1,0:T(8,128)(2,1)}, u32[]{:S(2)}) copy-start(bf16[1,384,1024]{2,1,0:T(8,128)(2,1)} %param.12) | copy-start | bytes 2359300
  66.2 8.3 %copy-start.6 = (bf16[512,384]{1,0:T(8,128)(2,1)S(1)}, bf16[512,384]{1,0:T(8,128)(2,1)}, u32[]{:S(2)}) copy-start(bf16[512,384]{1,0:T(8,128)(2,1)} %get-tuple-element.10) | copy-start | bytes 1179652
  70.0 18.8 %all-to-all-start.2 = ((bf16[4,2,65536]{2,1,0:T(2,128)(2,1)}), bf16[4,2,65536]{2,1,0:T(2,128)(2,1)}, u32[]{:S(2)}, u32[]{:S(2)}) async-start(bf16[4,2,65536]{2,1,0:T(2,128)(2,1)} %reshape.329), calls=%async_computation.2 | async-start | bytes 2097152 | tf_op jit(solution)/shard_map/all_to_all | solution.py:89
  84.7 7.9 %copy-start.8 = (s32[128,2]{0,1:T(2,128)S(1)}, s32[128,2]{0,1:T(2,128)}, u32[]{:S(2)}) copy-start(s32[128,2]{0,1:T(2,128)} %param.9) | copy-start | bytes 3076
  88.8 17.9 %all-to-all-start = ((bf16[4,2,65536]{2,1,0:T(2,128)(2,1)}), bf16[4,2,65536]{2,1,0:T(2,128)(2,1)S(1)}, u32[]{:S(2)}, u32[]{:S(2)}) async-start(bf16[4,2,65536]{2,1,0:T(2,128)(2,1)} %reshape.327), calls=%async_computation | async-start | bytes 2097152 | tf_op jit(solution)/shard_map/all_to_all | solution.py:86
Sparse Core Ops, SparseCore 0:
  50.0 67.0 reduce-scatter.2
  120.4 64.3 reduce-scatter.4
